TPU v7x, 32 devices: a whole 2x2x4 slice. The times are simulated.
32 devices in a mesh: dp: 1, seq: 32 (over z, y, x, core).
Axes of the slice: x: 2, y: 2, z: 4, core: 2. Of those that a mesh axis runs over, the one named last changes fastest.
Arguments:
- queries: bfloat16 [1, 1024, 6144], P('dp', None, 'seq'), may hold values from -360 to 360
- latent: bfloat16 [1, 1024, 576], P('dp', 'seq'), may hold values from -6 to 6
- latent_gain: float32 [512], replicated, may hold values from 0.1 to 1.9
- segments: int32 [1, 1024], P('dp', 'seq'), may hold values from 0 to 7, never falling along the last dimension, each value on 1 to 256 neighbouring positions
- up_weight: bfloat16 [512, 8192], P('dp', 'seq'), may hold values from -0.25 to 0.25
- out_grad: bfloat16 [1, 1024, 4096], P('dp', None, 'seq'), may hold values from -6 to 6
- hess_old: float32 [512, 8192], P('dp', 'seq'), may hold values from 0.01 to 0.3
Outputs:
- attn_out: bfloat16 [1, 1024, 4096], P('dp', None, 'seq')
- hess_new: float32 [512, 8192], P('dp', 'seq')
All inputs are finite; a program needn't handle non-finite values.
Results may differ from a plain program's by a relative error of at most 0.0075.
Values may be sent and summed in bfloat16 or wider, within the bound.
A program may use at most 64 MiB of HBM per device.

v0:
```python
import jax
import jax.numpy as jnp
from jax import lax
from jax.sharding import PartitionSpec as P

D_LAT = 512
D_ROPE = 64
D_NOPE = 128
D_VAL = 128


epsilon = 1e-06
ema_decay = 0.99
rope_base = 10000.0
masked_score = -1e30


def doc_positions(seg_ids):
    length = seg_ids.shape[0]
    places = jnp.arange(length, dtype=jnp.int32)
    starts_here = jnp.concatenate([jnp.ones((1,), dtype=bool), seg_ids[1:] != seg_ids[:-1]])
    starts = lax.cummax(jnp.where(starts_here, places, jnp.zeros_like(places)), axis=0)
    return places - starts


def rotate_pairs(values_in, positions):
    half_width = values_in.shape[-1] // 2
    steps_up = jnp.arange(half_width, dtype=jnp.float32)
    frequency = rope_base ** (-(2.0 * steps_up) / values_in.shape[-1])
    angles = positions.astype(jnp.float32)[:, None] * frequency[None, :]
    cosine = jnp.cos(angles)
    sine_term = jnp.sin(angles)
    first_half = values_in[:, :half_width]
    second = values_in[:, half_width:]
    return jnp.concatenate(
        [first_half * cosine - second * sine_term, second * cosine + first_half * sine_term], axis=1
    )


def normalize(latent_rows, latent_gain):
    compressed = latent_rows[:, :D_LAT].astype(jnp.float32)
    spread = jnp.mean(compressed * compressed, axis=-1, keepdims=True)
    return (compressed * lax.rsqrt(spread + epsilon) * latent_gain).astype(jnp.bfloat16)


def project_head(normed_seq, weight_head):
    key_nope = jnp.dot(
        normed_seq, weight_head[:, :D_NOPE], preferred_element_type=jnp.float32
    ).astype(jnp.bfloat16)
    value_rows = jnp.dot(
        normed_seq, weight_head[:, D_NOPE:], preferred_element_type=jnp.float32
    ).astype(jnp.bfloat16)
    return (key_nope, value_rows)


def block_allowed(places, seg_ids, first, lower, upper):
    causal = places[None, first:upper] <= places[lower:upper, None]
    same_doc = seg_ids[None, first:upper] == seg_ids[lower:upper, None]
    return causal & same_doc


def local(queries, latent, latent_gain, segments, up_weight, out_grad, hess_old):
    rope_raw = latent[:, :, D_LAT:]
    normed = normalize(latent[0], latent_gain)[None]
    gathered, rope_all, seg_all = (
        lax.all_gather(normed, "seq", axis=1, tiled=True),
        lax.all_gather(rope_raw, "seq", axis=1, tiled=True),
        lax.all_gather(segments, "seq", axis=1, tiled=True),
    )
    weight_full = lax.all_gather(up_weight, "dp", axis=0, tiled=True)
    seg_ids = seg_all[0]
    positions = doc_positions(seg_ids)
    normed_seq = gathered[0]
    key_rope = rotate_pairs(rope_all[0].astype(jnp.float32), positions).astype(jnp.bfloat16)
    length = seg_ids.shape[0]
    doc_reach = length // 4
    block_rows = min(512, length)
    count_blocks = length // block_rows
    firsts = [
        max(0, index * block_rows - (doc_reach - 1)) // 128 * 128 for index in range(count_blocks)
    ]
    places = jnp.arange(length, dtype=jnp.int32)
    score_scale = (D_NOPE + D_ROPE) ** (-0.5)
    query_rows = queries[0]
    grad_rows_in = out_grad[0]
    q_nope = query_rows[:, :D_NOPE]
    q_rope = rotate_pairs(query_rows[:, D_NOPE:].astype(jnp.float32), positions).astype(
        jnp.bfloat16
    )
    q_full = jnp.concatenate([q_nope, q_rope], axis=1)
    key_nope, value_rows = project_head(normed_seq, weight_full)
    key_full = jnp.concatenate([key_nope, key_rope], axis=1)
    pieces = []
    norm_pieces = []
    for query_block in range(count_blocks):
        lower = query_block * block_rows
        upper = lower + block_rows
        first = firsts[query_block]
        allowed = block_allowed(places, seg_ids, first, lower, upper)
        scores = (
            jnp.dot(
                q_full[lower:upper], key_full[first:upper].T, preferred_element_type=jnp.float32
            )
            * score_scale
        )
        scores = jnp.where(allowed, scores, masked_score)
        row_max = jnp.max(scores, axis=1, keepdims=True)
        expo_rows = jnp.where(allowed, jnp.exp(scores - row_max), 0.0)
        row_sum = jnp.sum(expo_rows, axis=1, keepdims=True)
        prob_low = (expo_rows / row_sum).astype(jnp.bfloat16)
        pieces.append(
            jnp.dot(prob_low, value_rows[first:upper], preferred_element_type=jnp.float32)
        )
        norm_pieces.append(row_max + jnp.log(row_sum))
    output = jnp.concatenate(pieces, axis=0)
    log_norm = jnp.concatenate(norm_pieces, axis=0)
    outputs = output.astype(jnp.bfloat16)
    key_again, value_back = project_head(normed_seq, weight_full)
    key_back = jnp.concatenate([key_again, key_rope], axis=1)
    delta_rows = jnp.sum(grad_rows_in.astype(jnp.float32) * output, axis=1, keepdims=True)
    value_grad = jnp.zeros((length, D_VAL), jnp.float32)
    key_grad = jnp.zeros((length, D_NOPE), jnp.float32)
    for query_block in range(count_blocks):
        lower = query_block * block_rows
        upper = lower + block_rows
        first = firsts[query_block]
        allowed = block_allowed(places, seg_ids, first, lower, upper)
        scores = (
            jnp.dot(
                q_full[lower:upper], key_back[first:upper].T, preferred_element_type=jnp.float32
            )
            * score_scale
        )
        scores = jnp.where(allowed, scores, masked_score)
        prob_rows = jnp.where(allowed, jnp.exp(scores - log_norm[lower:upper]), 0.0)
        prob_low = prob_rows.astype(jnp.bfloat16)
        grad_block = grad_rows_in[lower:upper]
        value_grad = value_grad.at[first:upper].add(
            jnp.dot(prob_low.T, grad_block, preferred_element_type=jnp.float32)
        )
        prob_grad = jnp.dot(
            grad_block, value_back[first:upper].T, preferred_element_type=jnp.float32
        )
        score_grad = (prob_rows * (prob_grad - delta_rows[lower:upper])).astype(jnp.bfloat16)
        key_grad = key_grad.at[first:upper].add(
            jnp.dot(score_grad.T, q_nope[lower:upper], preferred_element_type=jnp.float32)
        )
    key_low = (key_grad * score_scale).astype(jnp.bfloat16)
    value_low = value_grad.astype(jnp.bfloat16)
    columns = jnp.concatenate([key_low, value_low], axis=1)
    attn_out = outputs[None]
    grad_local = jnp.dot(normed_seq.T, columns, preferred_element_type=jnp.float32)
    grad_rows = lax.psum_scatter(grad_local, "dp", scatter_dimension=0, tiled=True)
    hess_new = ema_decay * hess_old + (1.0 - ema_decay) * grad_rows * grad_rows
    return (attn_out, hess_new)


def solution(mesh):
    return jax.shard_map(
        local,
        mesh=mesh,
        in_specs=(
            P("dp", None, "seq"),
            P("dp", "seq", None),
            P(),
            P("dp", "seq"),
            P("dp", "seq"),
            P("dp", None, "seq"),
            P("dp", "seq"),
        ),
        out_specs=(P("dp", None, "seq"), P("dp", "seq")),
        check_vma=False,
    )
```

profile of v0, /device:TPU:0, one launch (start us, length us, event | category | flops | bytes accessed | tf_op | source)
XLA Modules:
  0.0 122.4 jit_solution(9500552983791769979)
XLA Ops:
  7.2 0.9 fusion.79
  8.1 1.5 %fusion.81 = bf16[32,512]{1,0:T(8,128)(2,1)} fusion(f32[512]{0:T(512)} %param.17, f32[32]{0:T(128)S(1)} %add_rsqrt_fusion, bf16[32,576]{1,0:T(8,128)(2,1)} %bitcast.63), kind=kLoop, calls=%fused_computation.100 | loop fusion | flops 65536 | bytes 67712 | tf_op jit(solution)/shard_map/convert_element_type | solution.py:43
  9.6 0.7 slice.213
  10.3 0.7 bitcast_dynamic-update-slice_fusion
  11.1 41.9 %all-reduce.2 = s32[1024]{0:T(1024)S(1)} all-reduce(s32[1024]{0:T(1024)S(1)} %bitcast_dynamic-update-slice_fusion), channel_id=1, replica_groups=mesh['dp'=1,'seq'=32] {'seq'}, use_global_device_ids=true, to_apply=%add.2 | all-reduce | flops 1024 | bytes 8192
  53.6 41.0 %all_gather.12 = bf16[1,1024,64]{2,1,0:T(8,128)(2,1)S(1)} all-gather(bf16[1,32,64]{2,1,0:T(8,128)(2,1)S(1)} %slice.213), channel_id=1, replica_groups=mesh['dp'=1,'seq'=32] {'seq'}, dimensions={1}, use_global_device_ids=true | all-gather | bytes 135168 | tf_op jit(solution)/shard_map/all_gather | solution.py:67
  94.7 1.0 slice.237
  95.9 0.9 slice_convert_fusion
  96.9 0.6 fusion.53
  97.6 1.7 %convolution_convert_fusion.1 = bf16[1024,128]{0,1:T(8,128)(2,1)S(1)} fusion(bf16[1024,512]{1,0:T(8,128)(2,1)} %all-gather.3.cloned.1.call-done, bf16[512,256]{1,0:T(8,128)(2,1)S(1)} %copy-done.5), kind=kOutput, calls=%fused_computation.16 | convolution fusion | flops 134348800 | bytes 1441792 | tf_op jit(solution)/shard_map/dot_general | solution.py:47
  99.3 0.6 fusion.92
  100.0 0.6 fusion.10
  100.6 0.6 copy-done
  101.7 0.7 fusion.18
  102.3 0.4 fusion.93
  103.1 0.6 fusion.36
  104.3 1.2 fusion.21
  105.5 2.6 %fusion.6 = f32[512,128]{0,1:T(8,128)} fusion(f32[512,512]{0,1:T(8,128)} %copy-done.1, f32[512]{0:T(512)S(1)} %get-tuple-element.57, f32[512]{0:T(512)S(1)} %get-tuple-element.66, s32[512]{0:T(512)S(1)} %bitcast.71, s32[512]{0:T(512)S(1)} %slice.200, bf16[1024,192]{0,1:T(8,128)(2,1)} %bitcast.60, bf16[1024,128]{1,0:T(8,128)(2,1)S(1)} %convolution_convert_fusion, ...), kind=kOutput, calls=%fused_computation.14 | convolution fusion | flops 136314880 | bytes 1716224 | tf_op jit(solution)/shard_map/dot_general | solution.py:146
  108.1 1.0 scatter-add.16
  109.1 0.6 fusion.9
  109.7 0.7 convert_element_type.88
  110.5 1.9 %fusion.8 = f32[1024,128]{0,1:T(8,128)S(1)} fusion(f32[1024,128]{0,1:T(8,128)S(1)} %scatter-add.14, f32[512,768]{1,0:T(8,128)S(1)} %get-tuple-element.61, f32[512]{0:T(512)S(1)} %get-tuple-element.56, f32[512]{0:T(512)S(1)} %log_add_fusion, bf16[1024,128]{1,0:T(8,128)(2,1)} %copy-done.3, bf16[1024,192]{0,1:T(8,128)(2,1)} %bitcast.61, ...), kind=kOutput, calls=%fused_computation.18 | convolution fusion | flops 204570624 | bytes 2834432 | tf_op jit(solution)/shard_map/dot_general | solution.py:146
  112.5 0.7 pad_maximum_fusion.2
  113.2 2.4 %fusion.23 = f32[512,256]{1,0:T(8,128)} fusion(bf16[1024,512]{1,0:T(8,128)(2,1)S(1)} %copy-done, bf16[1024,128]{0,1:T(8,128)(2,1)} %convert_element_type.88, bf16[1024,128]{0,1:T(8,128)(2,1)S(1)} %multiply_convert_fusion, f32[512,256]{1,0:T(8,128)} %param.21), kind=kOutput, calls=%fused_computation.37 | convolution fusion | flops 270008320 | bytes 2621440 | tf_op jit(solution)/shard_map/dot_general | solution.py:152
  (45 shorter events, 2.7 us)
Async XLA Ops:
  7.2 90.4 %all-gather.3.cloned.1.call-start = ((), (), s32[]{:S(2)}) async-start(), calls=%async_computation | async-start | bytes 1081344 | tf_op jit(solution)/shard_map/all_gather | solution.py:66
  94.6 3.0 %copy-start.5 = (bf16[512,256]{1,0:T(8,128)(2,1)S(1)}, bf16[512,256]{1,0:T(8,128)(2,1)}, u32[]{:S(2)}) copy-start(bf16[512,256]{1,0:T(8,128)(2,1)} %param.19) | copy-start | bytes 786436
  99.9 1.2 %copy-start = (bf16[1024,512]{1,0:T(8,128)(2,1)S(1)}, bf16[1024,512]{1,0:T(8,128)(2,1)}, u32[]{:S(2)}) copy-start(bf16[1024,512]{1,0:T(8,128)(2,1)} %all-gather.3.cloned.1.call-done) | copy-start | bytes 3145732
  99.9 1.3 %copy-start.6 = (bf16[512,256]{1,0:T(8,128)(2,1)S(1)}, bf16[512,256]{1,0:T(8,128)(2,1)}, u32[]{:S(2)}) copy-start(bf16[512,256]{1,0:T(8,128)(2,1)} %param.19) | copy-start | bytes 786436
  101.6 3.9 %copy-start.3 = (bf16[1024,128]{1,0:T(8,128)(2,1)}, bf16[1024,128]{1,0:T(8,128)(2,1)S(1)}, u32[]{:S(2)}) copy-start(bf16[1024,128]{1,0:T(8,128)(2,1)S(1)} %convolution_convert_fusion) | copy-start | bytes 786436
  102.7 1.6 %copy-start.1 = (f32[512,512]{0,1:T(8,128)}, f32[512,512]{0,1:T(8,128)S(1)}, u32[]{:S(2)}) copy-start(f32[512,512]{0,1:T(8,128)S(1)} %get-tuple-element.63) | copy-start | bytes 3145732
  103.1 1.0 copy-start.2
  109.1 1.4 %copy-start.4 = (f32[512,128]{0,1:T(8,128)S(1)}, f32[512,128]{0,1:T(8,128)}, u32[]{:S(2)}) copy-start(f32[512,128]{0,1:T(8,128)} %fusion.6) | copy-start | bytes 786436
Sparse Core Ops, SparseCore 0:
  11.4 56.5 all-gather.2
where the time goes:
time: 123 us; the launch traced here: 122 us
  blocking collectives  82.9 us (67%)
  between operations  14.3 us (12%)
  matrix products  13.1 us (11%)
  other arithmetic  7.21 us (6%)
  local copies, waits for them, and re-layouts  4.85 us (4%)
    unnamed x1, blocking collectives  41.9 us
    all_gather x1, blocking collectives, local(): lax.all_gather(rope_raw, 'seq', axis=1, tiled=True)  41 us
    dot_general x2, matrix products, local(): jnp.dot(score_grad.T, q_nope[lower:upper], preferred_element_type=jnp.flo...  4.47 us
  transfers between devices with their start and end apart: 1, of which 0 were waited for; matrix products, arithmetic and copies ran while one was open for 4% of the time, Pallas kernels for 0%

commit v1 on v0

v1 whole, which is shorter than its diff:
```python
import functools
import math

import jax
import jax.numpy as jnp
import numpy as np
from jax import lax
from jax.experimental import pallas as pl
from jax.experimental.pallas import tpu as pltpu
from jax.sharding import PartitionSpec as P

D_LAT = 512
D_ROPE = 64
D_NOPE = 128
D_VAL = 128
LANES = 128
PACK = D_LAT + LANES

epsilon = 1e-06
ema_decay = 0.99
rope_base = 10000.0
masked_score = -1e30
MESH = pl.DeviceIdType.MESH


def rope_table(reach):
    half = D_ROPE // 2
    steps_up = np.arange(half, dtype=np.float32)
    frequency = np.float32(rope_base) ** (-(np.float32(2.0) * steps_up) / np.float32(D_ROPE))
    angles = np.arange(reach, dtype=np.float32)[:, None] * frequency.astype(np.float32)[None, :]
    cosine = np.cos(angles.astype(np.float64)).astype(np.float32)
    sine = np.sin(angles.astype(np.float64)).astype(np.float32)
    whole = np.concatenate([cosine, cosine, -sine, sine], axis=1)
    parts = []
    for _ in range(3):
        part = whole.astype(jnp.bfloat16)
        parts.append(part)
        whole = whole - part.astype(np.float32)
    return np.stack(parts)


def swap_matrix():
    matrix = np.zeros((LANES, LANES), np.float32)
    for i in range(D_ROPE):
        matrix[i, i] = 1.0
        matrix[i, D_ROPE + (i + D_ROPE // 2) % D_ROPE] = 1.0
    return matrix.astype(jnp.bfloat16)


def mm(a, b):
    return jnp.dot(a, b, preferred_element_type=jnp.float32)


def mm_t(a, b):
    return lax.dot_general(a, b, (((1,), (1,)), ((), ())), preferred_element_type=jnp.float32)


def kernel(
    n,
    q_ref,
    lat_ref,
    gain_ref,
    seg_ref,
    w_ref,
    g_ref,
    table_ref,
    swap_ref,
    out_ref,
    grad_ref,
    buf,
    kfull,
    qfull,
    vals,
    vals_t,
    ends,
    g_t,
    q_t,
    acc,
    send_sem,
    recv_sem,
    fsend_sem,
    frecv_sem,
):
    me = lax.axis_index("seq")
    chips = n // 2
    chip = me // 2
    core = lax.rem(me, 2)
    sibling = chip * 2 + (1 - core)
    rows = lat_ref.shape[0]
    length = buf.shape[0]
    reach = table_ref.shape[1]

    def peer(step):
        return lax.rem(chip + step, chips) * 2 + core

    barrier = pltpu.get_barrier_semaphore()

    def greet(step, carry):
        pl.semaphore_signal(barrier, inc=1, device_id={"seq": peer(step)}, device_id_type=MESH)
        return carry

    lax.fori_loop(1, chips, greet, 0)
    pl.semaphore_signal(barrier, inc=1, device_id={"seq": sibling}, device_id_type=MESH)

    def block(owner):
        return buf.at[pl.ds(pl.multiple_of(owner * rows, rows), rows), :]

    compressed = lat_ref[:, :D_LAT].astype(jnp.float32)
    spread = jnp.mean(compressed * compressed, axis=-1, keepdims=True)
    normed = (compressed * lax.rsqrt(spread + epsilon) * gain_ref[...]).astype(jnp.bfloat16)
    mine = pl.ds(pl.multiple_of(me * rows, rows), rows)
    buf[mine, :D_LAT] = normed
    tail = jnp.concatenate(
        [
            lat_ref[:, D_LAT:],
            jnp.broadcast_to(seg_ref[...].astype(jnp.float32), (rows, LANES - D_ROPE)).astype(
                jnp.bfloat16
            ),
        ],
        axis=1,
    )
    buf[mine, D_LAT:] = tail

    pl.semaphore_wait(barrier, chips)

    def direct(step):
        return pltpu.make_async_remote_copy(
            src_ref=block(me),
            dst_ref=block(me),
            send_sem=send_sem.at[step],
            recv_sem=recv_sem.at[step],
            device_id={"seq": peer(step)},
            device_id_type=MESH,
        )

    def forward(step):
        owner = lax.rem(chip + chips - step, chips) * 2 + core
        return pltpu.make_async_remote_copy(
            src_ref=block(owner),
            dst_ref=block(owner),
            send_sem=fsend_sem.at[step],
            recv_sem=frecv_sem.at[step],
            device_id={"seq": sibling},
            device_id_type=MESH,
        )

    def launch(step, carry):
        direct(step).start()
        return carry

    lax.fori_loop(1, chips, launch, 0)
    forward(0).start()

    g_t[...] = g_ref[...].astype(jnp.float32).T.astype(jnp.bfloat16)
    q_t[...] = q_ref[:, :D_NOPE].astype(jnp.float32).T.astype(jnp.bfloat16)
    weight_v_t = w_ref[:, D_NOPE:].astype(jnp.float32).T.astype(jnp.bfloat16)

    def relay(step, carry):
        direct(step).wait_recv()
        forward(step).start()
        return carry

    lax.fori_loop(1, chips, relay, 0)

    def arrive(step, carry):
        forward(step).wait_recv()
        return carry

    lax.fori_loop(0, chips, arrive, 0)

    lane_seg = buf[:, D_LAT:].astype(jnp.float32)
    spare = pltpu.roll(lane_seg, D_ROPE, 1)
    lane = lax.broadcasted_iota(jnp.int32, (length, LANES), 1)
    seg_all = jnp.where(lane < D_ROPE, spare, lane_seg)
    lane_f = lane.astype(jnp.float32)
    before = jnp.sum(jnp.where(seg_all < lane_f, 1.0, 0.0), axis=0, keepdims=True)
    within = jnp.sum(jnp.where(seg_all <= lane_f, 1.0, 0.0), axis=0, keepdims=True)
    counts = jnp.concatenate(
        [
            jnp.broadcast_to(before, (LANES, LANES)).T,
            jnp.broadcast_to(within, (LANES, LANES)).T,
        ],
        axis=1,
    )
    high = jnp.floor(counts * (1.0 / 256.0)) * 256.0
    low = (counts - high).astype(jnp.bfloat16)
    high = high.astype(jnp.bfloat16)
    member = jnp.where(seg_all == lane_f, 1.0, 0.0).astype(jnp.bfloat16)
    bounds = mm(member, high) + mm(member, low)
    ends[...] = bounds[:, LANES:]
    token = lax.broadcasted_iota(jnp.int32, (length, LANES), 0).astype(jnp.float32)
    position = token - bounds[:, :LANES]
    columns = []
    for base in range(0, reach, LANES):
        columns.append(jnp.where(position == lane_f + float(base), 1.0, 0.0).astype(jnp.bfloat16))
    spot = jnp.concatenate(columns, axis=1)
    turn = mm(spot, table_ref[0]) + mm(spot, table_ref[1]) + mm(spot, table_ref[2])

    def rotate(pair):
        product = pair * turn
        return product + pltpu.roll(product, D_ROPE, 1)

    keep = lane < D_ROPE
    kfull[:, D_NOPE:] = rotate(mm(buf[:, D_LAT:], swap_ref[...])).astype(jnp.bfloat16)
    qfull[:, :D_NOPE] = q_ref[:, :D_NOPE]
    q_pair = mm(q_ref[:, D_NOPE:], swap_ref[:D_ROPE, :])
    qfull[:, D_NOPE:] = jnp.where(keep, rotate(q_pair), 0.0).astype(jnp.bfloat16)

    projected = mm(buf[:, :D_LAT], w_ref[...])
    kfull[:, :D_NOPE] = projected[:, :D_NOPE].astype(jnp.bfloat16)
    vals[...] = projected[:, D_NOPE:].astype(jnp.bfloat16)
    vals_t[...] = mm_t(weight_v_t, buf[:, :D_LAT]).astype(jnp.bfloat16)

    score_scale = (D_NOPE + D_ROPE) ** (-0.5)
    exponent_scale = score_scale * math.log2(math.e)
    acc[...] = jnp.zeros_like(acc)
    step_rows = LANES
    for lower in range(0, length, step_rows):
        upper = lower + step_rows
        first = max(0, lower - (reach - 1)) // LANES * LANES
        span = upper - first
        scores = mm_t(kfull[first:upper, :], qfull[lower:upper, :])
        key_at = lax.broadcasted_iota(jnp.int32, (span, step_rows), 0) + first
        query_at = lax.broadcasted_iota(jnp.int32, (span, step_rows), 1) + lower
        allowed = (query_at >= key_at) & (query_at.astype(jnp.float32) < ends[first:upper, :])
        scores = jnp.where(allowed, scores, masked_score)
        top = jnp.max(scores, axis=0, keepdims=True)
        expo = jnp.exp2((scores - top) * exponent_scale)
        total = jnp.sum(expo, axis=0, keepdims=True)
        prob = expo * (1.0 / total)
        prob_low = prob.astype(jnp.bfloat16)
        prob_grad = mm_t(vals[first:upper, :], g_ref[lower:upper, :])
        delta = jnp.sum(prob_low.astype(jnp.float32) * prob_grad, axis=0, keepdims=True)
        score_grad = (prob * (prob_grad - delta)).astype(jnp.bfloat16)
        output_t = mm(vals_t[:, first:upper], prob_low)
        out_ref[lower:upper, :] = output_t.T.astype(jnp.bfloat16)
        acc[:D_NOPE, first:upper] += mm_t(q_t[:, lower:upper], score_grad)
        acc[D_NOPE:, first:upper] += mm_t(g_t[:, lower:upper], prob_low)

    key_low = (acc[:D_NOPE, :] * score_scale).astype(jnp.bfloat16)
    value_low = acc[D_NOPE:, :].astype(jnp.bfloat16)
    columns_t = jnp.concatenate([key_low, value_low], axis=0)
    grad_ref[...] = mm(columns_t, buf[:, :D_LAT]).T

    def drain(step, carry):
        direct(step).wait_send()
        forward(step).wait_send()
        return carry

    forward(0).wait_send()
    lax.fori_loop(1, chips, drain, 0)


def local(n, copies, queries, latent, latent_gain, segments, up_weight, out_grad, hess_old):
    weight = up_weight
    if copies > 1:
        weight = lax.all_gather(up_weight, "dp", axis=0, tiled=True)
    length = queries.shape[1]
    reach = length // 4
    chips = n // 2
    table = jnp.asarray(rope_table(reach))
    swap = jnp.asarray(swap_matrix())
    vmem = pl.BlockSpec(memory_space=pltpu.VMEM)
    attn, gradient = pl.pallas_call(
        functools.partial(kernel, n),
        out_shape=(
            jax.ShapeDtypeStruct((length, D_VAL), jnp.bfloat16),
            jax.ShapeDtypeStruct((D_LAT, D_NOPE + D_VAL), jnp.float32),
        ),
        in_specs=[vmem] * 8,
        out_specs=(vmem, vmem),
        scratch_shapes=[
            pltpu.VMEM((length, PACK), jnp.bfloat16),
            pltpu.VMEM((length, 2 * LANES), jnp.bfloat16),
            pltpu.VMEM((length, 2 * LANES), jnp.bfloat16),
            pltpu.VMEM((length, D_VAL), jnp.bfloat16),
            pltpu.VMEM((D_VAL, length), jnp.bfloat16),
            pltpu.VMEM((length, LANES), jnp.float32),
            pltpu.VMEM((D_VAL, length), jnp.bfloat16),
            pltpu.VMEM((D_NOPE, length), jnp.bfloat16),
            pltpu.VMEM((D_NOPE + D_VAL, length), jnp.float32),
            pltpu.SemaphoreType.DMA((chips,)),
            pltpu.SemaphoreType.DMA((chips,)),
            pltpu.SemaphoreType.DMA((chips,)),
            pltpu.SemaphoreType.DMA((chips,)),
        ],
        compiler_params=pltpu.CompilerParams(
            collective_id=0, has_side_effects=True, vmem_limit_bytes=48 << 20
        ),
    )(
        queries[0],
        latent[0],
        latent_gain[None, :],
        segments[0][:, None],
        weight,
        out_grad[0],
        table,
        swap,
    )
    if copies > 1:
        gradient = lax.psum_scatter(gradient, "dp", scatter_dimension=0, tiled=True)
    hess_new = ema_decay * hess_old + (1.0 - ema_decay) * gradient * gradient
    return (attn[None], hess_new)


def solution(mesh):
    return jax.shard_map(
        functools.partial(local, mesh.shape["seq"], mesh.shape["dp"]),
        mesh=mesh,
        in_specs=(
            P("dp", None, "seq"),
            P("dp", "seq", None),
            P(),
            P("dp", "seq"),
            P("dp", "seq"),
            P("dp", None, "seq"),
            P("dp", "seq"),
        ),
        out_specs=(P("dp", None, "seq"), P("dp", "seq")),
        check_vma=False,
    )
```

time: 123 us -> 32.4 us (0.26)
  the two profiles are of different devices: /device:TPU:0 before, /device:TPU:29 now
where the time goes in v1:
time: 32.4 us; the launch traced here: 32.3 us
  Pallas kernels  27.9 us (86%)
  local copies, waits for them, and re-layouts  2.74 us (8%)
  other arithmetic  0.88 us (3%)
  between operations  0.74 us (2%)
    pallas_call x1, Pallas kernels, local(): pl.pallas_call(functools.partial(kernel, n), out_shape=(jax.ShapeDtypeStr...  27.9 us
    unnamed x18, local copies, waits for them, and re-layouts  2.65 us
    add x1, other arithmetic, local(): hess_new = ema_decay * hess_old + (1.0 - ema_decay) * gradient * gradient  0.88 us

profile of v1, /device:TPU:29, one launch (start us, length us, event | category | flops | bytes accessed | tf_op | source)
XLA Modules:
  0.0 32.3 jit_solution(1139672901690466347)
XLA Ops:
  0.6 0.0 copy-start.7
  0.6 0.6 %copy-done.7 = s32[1,32]{1,0:T(1,128)S(1)} copy-done((s32[1,32]{1,0:T(1,128)S(1)}, s32[1,32]{1,0:T(1,128)}, u32[]{:S(2)}) %copy-start.7) | copy-done | bytes 152
  1.3 0.1 copy.12.seg_ref
  1.4 0.0 copy-start
  1.4 0.0 copy-start.1
  1.4 0.0 copy-start.2
  1.4 0.0 copy-start.3
  1.4 0.0 copy-start.4
  1.4 0.0 copy-start.5
  1.4 1.3 %copy.11 = bf16[1,1024,192]{2,1,0:T(8,128)(2,1)S(1)} copy(bf16[1,1024,192]{1,2,0:T(8,128)(2,1)} %param.9) | data formatting | bytes 786432 | tf_op args[0]
  2.7 0.0 copy-done
  2.7 0.0 copy-done.1
  2.7 0.0 copy-done.2
  2.7 0.0 copy-done.3
  2.7 0.0 copy-done.4
  2.7 0.0 copy-done.5
  2.7 0.0 copy-start.6
  2.8 27.9 %shard_map.104 = (bf16[1024,128]{1,0:T(8,128)(2,1)S(1)}, f32[512,256]{1,0:T(8,128)S(1)}) custom-call(bf16[1024,192]{1,0:T(8,128)(2,1)S(1)} %bitcast.6, bf16[32,576]{1,0:T(8,128)(2,1)S(1)} %bitcast.9, f32[1,512]{1,0:T(1,128)S(1)} %bitcast.10, s32[32,1]{1,0:T(8,128)S(1)} %copy.12.seg_ref, bf16[512,256]{1,0:T(8,128)(2,1)S(1)} %copy-done, ...), custom_call_target="tpu_custom_call" | custom-call | tf_op jit(solution)/shard_map/pallas_call | solution.py:264
  30.7 0.0 copy-done.6
  30.7 0.9 %fusion = f32[512,256]{1,0:T(8,128)} fusion(f32[512,256]{1,0:T(8,128)S(1)} %get-tuple-element.5, f32[512,256]{1,0:T(8,128)S(1)} %copy-done.6), kind=kLoop, calls=%fused_computation.1 | loop fusion | flops 524288 | bytes 1572864 | tf_op jit(solution)/shard_map/add | solution.py:302
  31.6 0.7 %copy.14 = bf16[1,1024,128]{2,1,0:T(8,128)(2,1)} copy(bf16[1,1024,128]{2,1,0:T(8,128)(2,1)S(1)} %bitcast.7) | data formatting | bytes 524288
Async XLA Ops:
  0.6 0.7 %copy-start.7 = (s32[1,32]{1,0:T(1,128)S(1)}, s32[1,32]{1,0:T(1,128)}, u32[]{:S(2)}) copy-start(s32[1,32]{1,0:T(1,128)} %param.12) | copy-start | bytes 388
  1.4 1.3 %copy-start = (bf16[512,256]{1,0:T(8,128)(2,1)S(1)}, bf16[512,256]{1,0:T(8,128)(2,1)}, u32[]{:S(2)}) copy-start(bf16[512,256]{1,0:T(8,128)(2,1)} %w_ref.1) | copy-start | bytes 786436
  1.4 1.3 %copy-start.1 = (bf16[1,1024,128]{2,1,0:T(8,128)(2,1)S(1)}, bf16[1,1024,128]{2,1,0:T(8,128)(2,1)}, u32[]{:S(2)}) copy-start(bf16[1,1024,128]{2,1,0:T(8,128)(2,1)} %param.14) | copy-start | bytes 786436
  1.4 1.3 %copy-start.2 = (bf16[3,256,128]{2,1,0:T(8,128)(2,1)S(1)}, bf16[3,256,128]{2,1,0:T(8,128)(2,1)}, u32[]{:S(2)}) copy-start(bf16[3,256,128]{2,1,0:T(8,128)(2,1)} %constant.8.clone.table_ref) | copy-start | bytes 589828
  1.4 1.3 %copy-start.3 = (bf16[1,32,576]{2,1,0:T(8,128)(2,1)S(1)}, bf16[1,32,576]{2,1,0:T(8,128)(2,1)}, u32[]{:S(2)}) copy-start(bf16[1,32,576]{2,1,0:T(8,128)(2,1)} %param.10) | copy-start | bytes 110596
  1.4 1.3 %copy-start.4 = (bf16[128,128]{1,0:T(8,128)(2,1)S(1)}, bf16[128,128]{1,0:T(8,128)(2,1)}, u32[]{:S(2)}) copy-start(bf16[128,128]{1,0:T(8,128)(2,1)} %constant.9.clone.swap_ref) | copy-start | bytes 98308
  1.4 1.3 %copy-start.5 = (f32[512]{0:T(512)S(1)}, f32[512]{0:T(512)}, u32[]{:S(2)}) copy-start(f32[512]{0:T(512)} %param.11) | copy-start | bytes 6148
  2.7 28.0 %copy-start.6 = (f32[512,256]{1,0:T(8,128)S(1)}, f32[512,256]{1,0:T(8,128)}, u32[]{:S(2)}) copy-start(f32[512,256]{1,0:T(8,128)} %param.15) | copy-start | bytes 1572868

commit v2 on v1

v2 whole, which is shorter than its diff:
```python
import functools
import math

import jax
import jax.numpy as jnp
import numpy as np
from jax import lax
from jax.experimental import pallas as pl
from jax.experimental.pallas import tpu as pltpu
from jax.sharding import PartitionSpec as P

D_LAT = 512
D_ROPE = 64
D_NOPE = 128
D_VAL = 128
LANES = 128
PACK = D_LAT + LANES
SIDE = 2

epsilon = 1e-06
ema_decay = 0.99
rope_base = 10000.0
masked_score = -1e30
MESH = pl.DeviceIdType.MESH


def rope_table(reach):
    half = D_ROPE // 2
    steps_up = np.arange(half, dtype=np.float32)
    frequency = np.float32(rope_base) ** (-(np.float32(2.0) * steps_up) / np.float32(D_ROPE))
    angles = np.arange(reach, dtype=np.float32)[:, None] * frequency.astype(np.float32)[None, :]
    cosine = np.cos(angles.astype(np.float64)).astype(np.float32)
    sine = np.sin(angles.astype(np.float64)).astype(np.float32)
    whole = np.concatenate([cosine, cosine, -sine, sine], axis=1)
    parts = []
    for _ in range(3):
        part = whole.astype(jnp.bfloat16)
        parts.append(part)
        whole = whole - part.astype(np.float32)
    return np.stack(parts)


def swap_matrix(shape, dim):
    entry = lax.broadcasted_iota(jnp.int32, shape, dim)
    place = lax.broadcasted_iota(jnp.int32, shape, 1 - dim)
    half = D_ROPE // 2
    partner = D_ROPE + jnp.where(entry < half, entry + half, entry - half)
    hit = (entry < D_ROPE) & ((place == entry) | (place == partner))
    return jnp.where(hit, 1.0, 0.0).astype(jnp.bfloat16)


def mm(a, b):
    return jnp.dot(a, b, preferred_element_type=jnp.float32)


def mm_t(a, b):
    return lax.dot_general(a, b, (((1,), (1,)), ((), ())), preferred_element_type=jnp.float32)


def kernel(
    n,
    q_hbm,
    lat_hbm,
    gain_hbm,
    seg_hbm,
    w_hbm,
    g_hbm,
    table_hbm,
    out_ref,
    grad_ref,
    q_ref,
    lat_ref,
    gain_ref,
    seg_ref,
    w_ref,
    g_ref,
    table_ref,
    buf,
    kfull,
    qfull_t,
    vals,
    vals_t,
    ends,
    g_t,
    weight_v_t,
    acc,
    send_sem,
    recv_sem,
    load_sem,
):
    me = lax.axis_index("seq")
    chip = me // 2
    core = lax.rem(me, 2)
    minor = lax.rem(chip, SIDE * SIDE)
    major = chip // (SIDE * SIDE)
    planes = n // (2 * SIDE * SIDE)
    minor_x = minor + 1 - 2 * lax.rem(minor, SIDE)
    minor_y = minor + SIDE - 2 * SIDE * (minor // SIDE)
    minor_d = minor_x + minor_y - minor

    def device(plane, place, side):
        return (plane * (SIDE * SIDE) + place) * 2 + side

    def plane_of(step):
        return lax.rem(major + planes + step, planes)

    sibling = device(major, minor, 1 - core)
    across_x = device(major, minor_x, core)
    across_y = device(major, minor_y, core)
    across_d = device(major, minor_d, core)
    partners = [sibling, across_x, across_y, across_d]
    partners += [device(plane_of(step), minor, core) for step in range(1, planes)]
    rows = lat_ref.shape[0]
    length = buf.shape[0]
    reach = table_ref.shape[1]

    pairs = (
        (lat_hbm, lat_ref),
        (gain_hbm, gain_ref),
        (seg_hbm, seg_ref),
        (g_hbm, g_ref),
        (w_hbm, w_ref),
        (q_hbm, q_ref),
        (table_hbm, table_ref),
    )
    loads = [
        pltpu.make_async_copy(source, target, load_sem.at[at])
        for at, (source, target) in enumerate(pairs)
    ]
    for load in loads[:3]:
        load.start()
    barrier = pltpu.get_barrier_semaphore()
    for partner in partners:
        pl.semaphore_signal(barrier, inc=1, device_id={"seq": partner}, device_id_type=MESH)

    def block(owner):
        return buf.at[pl.ds(pl.multiple_of(owner * rows, rows), rows), :]

    for load in loads[3:]:
        load.start()
    for load in loads[:3]:
        load.wait()
    compressed = lat_ref[:, :D_LAT].astype(jnp.float32)
    spread = jnp.mean(compressed * compressed, axis=-1, keepdims=True)
    normed = (compressed * lax.rsqrt(spread + epsilon) * gain_ref[...]).astype(jnp.bfloat16)
    mine = pl.ds(pl.multiple_of(me * rows, rows), rows)
    buf[mine, :D_LAT] = normed
    down = lax.broadcasted_iota(jnp.int32, (rows, rows), 0)
    right = lax.broadcasted_iota(jnp.int32, (rows, rows), 1)
    seg_column = jnp.sum(
        jnp.where(down == right, seg_ref[...].astype(jnp.float32), 0.0), axis=1, keepdims=True
    )
    seg_wide = jnp.broadcast_to(seg_column, (rows, LANES - D_ROPE)).astype(jnp.bfloat16)
    tail = jnp.concatenate([lat_ref[:, D_LAT:], seg_wide], axis=1)
    buf[mine, D_LAT:] = tail

    pl.semaphore_wait(barrier, len(partners))

    def send(owner, slot, target):
        return pltpu.make_async_remote_copy(
            src_ref=block(owner),
            dst_ref=block(owner),
            send_sem=send_sem.at[slot],
            recv_sem=recv_sem.at[slot],
            device_id={"seq": target},
            device_id_type=MESH,
        )

    places = (minor, minor_x, minor_y, minor_d)

    def along(step):
        return send(me, 8 * step, device(plane_of(step), minor, core))

    def over(way, step):
        owner = device(plane_of(-step), minor, core)
        return send(owner, 8 * step + 1 + way, (across_x, across_y, across_d)[way])

    def share(place, step):
        owner = device(plane_of(-step), places[place], core)
        return send(owner, 8 * step + 4 + place, sibling)

    started = []

    def begin(copy):
        copy.start()
        started.append(copy)

    order = sorted(range(1, planes), key=lambda step: (min(step, planes - step), step))
    for step in order:
        begin(along(step))
    for way in range(3):
        begin(over(way, 0))
    begin(share(0, 0))

    for load in loads[3:]:
        load.wait()
    g_t[...] = g_ref[...].astype(jnp.float32).T.astype(jnp.bfloat16)
    weight_v_t[...] = w_ref[:, D_NOPE:].astype(jnp.float32).T.astype(jnp.bfloat16)
    swap = swap_matrix((LANES, LANES), 0)
    swap_t = swap_matrix((LANES, D_ROPE), 1)
    qfull_t[:D_NOPE, :] = q_ref[:D_NOPE, :]
    qfull_t[D_NOPE + D_ROPE :, :] = jnp.zeros_like(qfull_t[D_NOPE + D_ROPE :, :])

    def crossed(step):
        for way in range(3):
            over(way, step).wait_recv()
            begin(share(1 + way, step))

    for step in order:
        along(step).wait_recv()
        for way in range(3):
            begin(over(way, step))
        begin(share(0, step))
        if step == order[0]:
            crossed(0)
    for step in order:
        crossed(step)

    plane_rows = 2 * SIDE * SIDE * rows
    for step in [0] + order:
        for place in range(4):
            share(place, step).wait_recv()
        here = pl.ds(pl.multiple_of(plane_of(-step) * plane_rows, plane_rows), plane_rows)
        arrived = buf[here, :D_LAT]
        projected = mm(arrived, w_ref[...])
        kfull[here, :D_NOPE] = projected[:, :D_NOPE].astype(jnp.bfloat16)
        vals[here, :] = projected[:, D_NOPE:].astype(jnp.bfloat16)
        vals_t[:, here] = mm_t(weight_v_t[...], arrived).astype(jnp.bfloat16)

    lane_seg = buf[:, D_LAT:].astype(jnp.float32)
    spare = pltpu.roll(lane_seg, D_ROPE, 1)
    lane = lax.broadcasted_iota(jnp.int32, (length, LANES), 1)
    seg_all = jnp.where(lane < D_ROPE, spare, lane_seg)
    lane_f = lane.astype(jnp.float32)
    before = jnp.sum(jnp.where(seg_all < lane_f, 1.0, 0.0), axis=0, keepdims=True)
    within = jnp.sum(jnp.where(seg_all <= lane_f, 1.0, 0.0), axis=0, keepdims=True)
    counts = jnp.concatenate(
        [
            jnp.broadcast_to(before, (LANES, LANES)).T,
            jnp.broadcast_to(within, (LANES, LANES)).T,
        ],
        axis=1,
    )
    high = jnp.floor(counts * (1.0 / 256.0)) * 256.0
    low = (counts - high).astype(jnp.bfloat16)
    high = high.astype(jnp.bfloat16)
    member = jnp.where(seg_all == lane_f, 1.0, 0.0).astype(jnp.bfloat16)
    bounds = mm(member, high) + mm(member, low)
    ends[...] = bounds[:, LANES:]
    token = lax.broadcasted_iota(jnp.int32, (length, LANES), 0).astype(jnp.float32)
    position = token - bounds[:, :LANES]
    columns = []
    for base in range(0, reach, LANES):
        columns.append(jnp.where(position == lane_f + float(base), 1.0, 0.0).astype(jnp.bfloat16))
    spot = jnp.concatenate(columns, axis=1)
    turn = mm(spot, table_ref[0]) + mm(spot, table_ref[1]) + mm(spot, table_ref[2])

    product = mm(buf[:, D_LAT:], swap) * turn
    kfull[:, D_NOPE:] = (product + pltpu.roll(product, D_ROPE, 1)).astype(jnp.bfloat16)
    product_t = mm(swap_t, q_ref[D_NOPE:, :]) * turn.T
    qfull_t[D_NOPE : D_NOPE + D_ROPE, :] = (product_t[:D_ROPE, :] + product_t[D_ROPE:, :]).astype(
        jnp.bfloat16
    )

    score_scale = (D_NOPE + D_ROPE) ** (-0.5)
    exponent_scale = score_scale * math.log2(math.e)
    acc[...] = jnp.zeros_like(acc)
    step_rows = LANES
    for lower in range(0, length, step_rows):
        upper = lower + step_rows
        first = max(0, lower - (reach - 1)) // LANES * LANES
        span = upper - first
        scores = mm(kfull[first:upper, :], qfull_t[:, lower:upper])
        key_at = lax.broadcasted_iota(jnp.int32, (span, step_rows), 0) + first
        query_at = lax.broadcasted_iota(jnp.int32, (span, step_rows), 1) + lower
        allowed = (query_at >= key_at) & (query_at.astype(jnp.float32) < ends[first:upper, :])
        scores = jnp.where(allowed, scores, masked_score)
        top = jnp.max(scores, axis=0, keepdims=True)
        expo = jnp.exp2((scores - top) * exponent_scale)
        total = jnp.sum(expo, axis=0, keepdims=True)
        prob = expo * (1.0 / total)
        prob_low = prob.astype(jnp.bfloat16)
        prob_grad = mm_t(vals[first:upper, :], g_ref[lower:upper, :])
        delta = jnp.sum(prob_low.astype(jnp.float32) * prob_grad, axis=0, keepdims=True)
        score_grad = (prob * (prob_grad - delta)).astype(jnp.bfloat16)
        output_t = mm(vals_t[:, first:upper], prob_low)
        out_ref[lower:upper, :] = output_t.T.astype(jnp.bfloat16)
        acc[:D_NOPE, first:upper] += mm_t(q_ref[:D_NOPE, lower:upper], score_grad)
        acc[D_NOPE:, first:upper] += mm_t(g_t[:, lower:upper], prob_low)

    key_low = (acc[:D_NOPE, :] * score_scale).astype(jnp.bfloat16)
    value_low = acc[D_NOPE:, :].astype(jnp.bfloat16)
    columns_t = jnp.concatenate([key_low, value_low], axis=0)
    grad_ref[...] = mm(columns_t, buf[:, :D_LAT]).T

    for copy in started:
        copy.wait_send()


def local(n, copies, queries, latent, latent_gain, segments, up_weight, out_grad, hess_old):
    weight = up_weight
    if copies > 1:
        weight = lax.all_gather(up_weight, "dp", axis=0, tiled=True)
    length = queries.shape[1]
    reach = length // 4
    slots = 8 * (n // (2 * SIDE * SIDE))
    table = jnp.asarray(rope_table(reach))
    operands = (
        queries[0].T,
        latent[0],
        latent_gain[None, :],
        segments,
        weight,
        out_grad[0],
        table,
    )
    vmem = pl.BlockSpec(memory_space=pltpu.VMEM)
    attn, gradient = pl.pallas_call(
        functools.partial(kernel, n),
        out_shape=(
            jax.ShapeDtypeStruct((length, D_VAL), jnp.bfloat16),
            jax.ShapeDtypeStruct((D_LAT, D_NOPE + D_VAL), jnp.float32),
        ),
        in_specs=[pl.BlockSpec(memory_space=pltpu.HBM)] * len(operands),
        out_specs=(vmem, vmem),
        scratch_shapes=[pltpu.VMEM(operand.shape, operand.dtype) for operand in operands]
        + [
            pltpu.VMEM((length, PACK), jnp.bfloat16),
            pltpu.VMEM((length, 2 * LANES), jnp.bfloat16),
            pltpu.VMEM((2 * LANES, length), jnp.bfloat16),
            pltpu.VMEM((length, D_VAL), jnp.bfloat16),
            pltpu.VMEM((D_VAL, length), jnp.bfloat16),
            pltpu.VMEM((length, LANES), jnp.float32),
            pltpu.VMEM((D_VAL, length), jnp.bfloat16),
            pltpu.VMEM((D_VAL, D_LAT), jnp.bfloat16),
            pltpu.VMEM((D_NOPE + D_VAL, length), jnp.float32),
            pltpu.SemaphoreType.DMA((slots,)),
            pltpu.SemaphoreType.DMA((slots,)),
            pltpu.SemaphoreType.DMA((len(operands),)),
        ],
        compiler_params=pltpu.CompilerParams(
            collective_id=0, has_side_effects=True
        ),
    )(*operands)
    if copies > 1:
        gradient = lax.psum_scatter(gradient, "dp", scatter_dimension=0, tiled=True)
    hess_new = ema_decay * hess_old + (1.0 - ema_decay) * gradient * gradient
    return (attn[None], hess_new)


def solution(mesh):
    return jax.shard_map(
        functools.partial(local, mesh.shape["seq"], mesh.shape["dp"]),
        mesh=mesh,
        in_specs=(
            P("dp", None, "seq"),
            P("dp", "seq", None),
            P(),
            P("dp", "seq"),
            P("dp", "seq"),
            P("dp", None, "seq"),
            P("dp", "seq"),
        ),
        out_specs=(P("dp", None, "seq"), P("dp", "seq")),
        check_vma=False,
    )
```

time: 32.4 us -> 27.3 us (0.84)
  the two profiles are of different devices: /device:TPU:29 before, /device:TPU:0 now
where the time goes in v2:
time: 27.3 us; the launch traced here: 27.2 us
  Pallas kernels  23.8 us (87%)
  other arithmetic  1.96 us (7%)
  local copies, waits for them, and re-layouts  0.71 us (3%)
  between operations  0.66 us (2%)
    pallas_call x1, Pallas kernels, local(): pl.pallas_call(functools.partial(kernel, n), out_shape=(jax.ShapeDtypeStr...  23.8 us
    add x1, other arithmetic, local(): hess_new = ema_decay * hess_old + (1.0 - ema_decay) * gradient * gradient  1.96 us
    unnamed x5, local copies, waits for them, and re-layouts  0.71 us

profile of v2, /device:TPU:0, one launch (start us, length us, event | category | flops | bytes accessed | tf_op | source)
XLA Modules:
  0.0 27.2 jit_solution(10167611487550818677)
XLA Ops:
  0.6 0.0 copy-start
  0.6 23.8 %shard_map.95 = (bf16[1024,128]{1,0:T(8,128)(2,1)}, f32[512,256]{1,0:T(8,128)}) custom-call(bf16[192,1024]{1,0:T(8,128)(2,1)} %bitcast.7, bf16[32,576]{1,0:T(8,128)(2,1)} %bitcast.10, f32[1,512]{1,0:T(1,128)} %bitcast.11, s32[1,32]{1,0:T(1,128)} %seg_hbm.1, bf16[512,256]{1,0:T(8,128)(2,1)} %w_hbm.1, bf16[1024,128]{1,0:T(8,128)(2,1)} %bitcast.9, ...), custom_call_target="tpu_custom_call" | custom-call | tf_op jit(solution)/shard_map/pallas_call | solution.py:318
  24.5 0.0 copy-done
  24.5 0.0 copy-start.1
  24.5 2.0 %fusion = f32[512,256]{1,0:T(8,128)} fusion(f32[512,256]{1,0:T(8,128)} %get-tuple-element.5, f32[512,256]{1,0:T(8,128)S(1)} %copy-done), kind=kLoop, calls=%fused_computation.1 | loop fusion | flops 524288 | bytes 1572864 | tf_op jit(solution)/shard_map/add | solution.py:347
  26.5 0.0 copy-done.1
  26.5 0.7 %copy.11 = bf16[1,1024,128]{2,1,0:T(8,128)(2,1)} copy(bf16[1,1024,128]{2,1,0:T(8,128)(2,1)S(1)} %bitcast.8) | data formatting | bytes 524288
Async XLA Ops:
  0.6 23.9 %copy-start = (f32[512,256]{1,0:T(8,128)S(1)}, f32[512,256]{1,0:T(8,128)}, u32[]{:S(2)}) copy-start(f32[512,256]{1,0:T(8,128)} %param.14) | copy-start | bytes 1572868
  24.5 2.0 %copy-start.1 = (bf16[1024,128]{1,0:T(8,128)(2,1)S(1)}, bf16[1024,128]{1,0:T(8,128)(2,1)}, u32[]{:S(2)}) copy-start(bf16[1024,128]{1,0:T(8,128)(2,1)} %get-tuple-element.4) | copy-start | bytes 786436
